TPU v7x, 512 devices: a whole 4x4x16 slice. The times are simulated.
512 devices in a mesh: seq: 64 (over z, x), head: 8 (over y, core).
Axes of the slice: x: 4, y: 4, z: 16, core: 2. Of those that a mesh axis runs over, the one named last changes fastest.
Arguments:
- queries: bfloat16 [16384, 8192], P(('seq', 'head')), may hold values from -6 to 6
- key_vectors: bfloat16 [16384, 8192], P(('seq', 'head')), may hold values from -6 to 6
- value_vectors: bfloat16 [16384, 8192], P(('seq', 'head')), may hold values from -6 to 6
- out_grad: bfloat16 [16384, 8192], P(('seq', 'head')), may hold values from -6 to 6
Outputs:
- query_grad: bfloat16 [16384, 8192], P(('seq', 'head'))
- key_grad: bfloat16 [16384, 8192], P(('seq', 'head'))
- value_grad: bfloat16 [16384, 8192], P(('seq', 'head'))
All inputs are finite; a program needn't handle non-finite values.
Results may differ from a plain program's by a relative error of at most 0.005.
Values may be sent and summed in bfloat16 or wider, within the bound.
No kernel may reach another device: no remote copies, remote signals or barrier semaphores. Data moves between devices by JAX's collectives and lax.ppermute only.
A program may use at most 192 MiB of HBM per device.

v0:
```python
import jax
import jax.numpy as jnp
from jax import lax
from jax.sharding import PartitionSpec as P

HEAD_DIM = 128


def carried_in(value, axis, combine, identity, reverse):
    peers, here = (lax.axis_size(axis), lax.axis_index(axis))
    everything = lax.all_gather(value, axis)
    start = jnp.broadcast_to(jnp.asarray(identity, value.dtype), value.shape)

    def turn(k, before):
        at = peers - 1 - k if reverse else k
        reached = at > here if reverse else at < here
        new = combine(before, everything[at])
        return jnp.where(reached, new, before)

    return lax.fori_loop(0, peers, turn, start)


def combine_sum(earlier, later):
    return jax.tree.map(jnp.add, earlier, later)


def local(queries, key_vectors, value_vectors, out_grad):
    f32 = jnp.float32
    hi = lax.Precision.HIGHEST
    groups = lax.axis_size("head")
    rows = queries.shape[0] * groups
    width = queries.shape[1] // groups
    heads = width // HEAD_DIM
    q_loc, k_loc, v_loc, g_loc = (
        lax.all_to_all(queries, "head", split_axis=1, concat_axis=0, tiled=True),
        lax.all_to_all(key_vectors, "head", split_axis=1, concat_axis=0, tiled=True),
        lax.all_to_all(value_vectors, "head", split_axis=1, concat_axis=0, tiled=True),
        lax.all_to_all(out_grad, "head", split_axis=1, concat_axis=0, tiled=True),
    )
    start = (lax.axis_index("seq") * rows).astype(f32)
    position = jnp.arange(rows, dtype=f32) + start
    factor = lax.rsqrt(HEAD_DIM * (position + 1.0))
    scaled = (g_loc.astype(f32) * factor[:, None]).astype(jnp.bfloat16)

    def head_major(x):
        return jnp.transpose(x.reshape(rows, heads, HEAD_DIM), (1, 0, 2))

    qh = head_major(q_loc)
    kh = head_major(k_loc)
    vh = head_major(v_loc)
    gh = head_major(scaled)
    kv_sum = jnp.einsum("htd,hte->hde", kh, vh, preferred_element_type=f32)
    qg_sum = jnp.einsum("htd,hte->hde", qh, gh, preferred_element_type=f32)
    zero_state = jnp.zeros((heads, HEAD_DIM, HEAD_DIM), f32)
    before = carried_in(kv_sum, "seq", combine_sum, zero_state, False)
    after = carried_in(qg_sum, "seq", combine_sum, zero_state, True)
    index = jnp.arange(rows, dtype=jnp.int32)
    keep = index[:, None] >= index[None, :]
    inner = jnp.where(
        keep[None], jnp.einsum("hte,hse->hts", gh, vh, preferred_element_type=f32), 0.0
    ).astype(jnp.bfloat16)
    pairs = jnp.where(
        keep[None], jnp.einsum("htd,hsd->hts", qh, kh, preferred_element_type=f32), 0.0
    ).astype(jnp.bfloat16)
    dq = jnp.einsum("hts,hsd->htd", inner, kh, preferred_element_type=f32) + jnp.einsum(
        "hte,hde->htd", gh.astype(f32), before, precision=hi
    )
    dk = jnp.einsum("hts,htd->hsd", inner, qh, preferred_element_type=f32) + jnp.einsum(
        "hse,hde->hsd", vh.astype(f32), after, precision=hi
    )
    dv = jnp.einsum("hts,hte->hse", pairs, gh, preferred_element_type=f32) + jnp.einsum(
        "hsd,hde->hse", kh.astype(f32), after, precision=hi
    )

    def token_major(x):
        return jnp.transpose(x.astype(jnp.bfloat16), (1, 0, 2)).reshape(rows, width)

    dq_loc = token_major(dq)
    dk_loc = token_major(dk)
    dv_loc = token_major(dv)
    query_grad, key_grad, value_grad = (
        lax.all_to_all(dq_loc, "head", split_axis=0, concat_axis=1, tiled=True),
        lax.all_to_all(dk_loc, "head", split_axis=0, concat_axis=1, tiled=True),
        lax.all_to_all(dv_loc, "head", split_axis=0, concat_axis=1, tiled=True),
    )
    return (query_grad, key_grad, value_grad)


def solution(mesh):
    placed = (
        P(("seq", "head"), None),
        P(("seq", "head"), None),
        P(("seq", "head"), None),
        P(("seq", "head"), None),
    )
    return jax.shard_map(
        local,
        mesh=mesh,
        in_specs=placed,
        out_specs=(P(("seq", "head"), None), P(("seq", "head"), None), P(("seq", "head"), None)),
        check_vma=False,
    )
```

profile of v0, /device:TPU:1, one launch (start us, length us, event | category | flops | bytes accessed | tf_op | source)
XLA Modules:
  0.0 733.2 jit_solution(7795061028266321221)
XLA Ops:
  7.2 1.9 copy.158
  9.1 10.2 %all-to-all-start = ((bf16[32,8,1024]{2,0,1:T(8,128)(2,1)}), bf16[32,8,1024]{2,0,1:T(8,128)(2,1)S(1)}, u32[]{:S(2)}, u32[]{:S(2)}) async-start(bf16[32,8,1024]{2,0,1:T(8,128)(2,1)} %bitcast.100), calls=%async_computation | async-start | bytes 1048576 | tf_op jit(solution)/shard_map/all_to_all | solution.py:38
  20.2 8.5 %all-to-all-done = bf16[32,8,1024]{2,0,1:T(8,128)(2,1)S(1)} async-done(((bf16[32,8,1024]{2,0,1:T(8,128)(2,1)}), bf16[32,8,1024]{2,0,1:T(8,128)(2,1)S(1)}, u32[]{:S(2)}, u32[]{:S(2)}) %all-to-all-start) | async-done | bytes 524320 | tf_op jit(solution)/shard_map/all_to_all | solution.py:38
  28.7 4.4 all-to-all-start.4
  33.4 9.0 %all-to-all-done.4 = bf16[32,8,1024]{2,0,1:T(8,128)(2,1)S(1)} async-done(((bf16[32,8,1024]{2,0,1:T(8,128)(2,1)}), bf16[32,8,1024]{2,0,1:T(8,128)(2,1)S(1)}, u32[]{:S(2)}, u32[]{:S(2)}) %all-to-all-start.4) | async-done | bytes 524320 | tf_op jit(solution)/shard_map/all_to_all | solution.py:35
  45.1 4.4 all-to-all-start.2
  50.3 8.5 %all-to-all-done.2 = bf16[32,8,1024]{2,0,1:T(8,128)(2,1)S(1)} async-done(((bf16[32,8,1024]{2,0,1:T(8,128)(2,1)}), bf16[32,8,1024]{2,0,1:T(8,128)(2,1)S(1)}, u32[]{:S(2)}, u32[]{:S(2)}) %all-to-all-start.2) | async-done | bytes 524320 | tf_op jit(solution)/shard_map/all_to_all | solution.py:36
  58.9 4.4 all-to-all-start.1
  63.4 9.3 %all-to-all-done.1 = bf16[32,8,1024]{2,0,1:T(8,128)(2,1)S(1)} async-done(((bf16[32,8,1024]{2,0,1:T(8,128)(2,1)}), bf16[32,8,1024]{2,0,1:T(8,128)(2,1)S(1)}, u32[]{:S(2)}, u32[]{:S(2)}) %all-to-all-start.1) | async-done | bytes 524320 | tf_op jit(solution)/shard_map/all_to_all | solution.py:37
  75.4 1.5 convolution_bitcast_fusion.2
  76.9 258.3 %all-gather.7.cloned.1.call-done = f32[512,128,128]{2,1,0:T(8,128)} async-done(((f32[8,128,128]{2,1,0:T(8,128)}), f32[512,128,128]{2,1,0:T(8,128)}) %all-gather.7.cloned.1.call-update) | async-done | bytes 33554448 | tf_op jit(solution)/shard_map/all_gather | solution.py:11
  335.2 80.6 %while.31 = (s32[]{:T(128)}, f32[8,128,128]{2,1,0:T(8,128)S(1)}, s32[]{:T(128)}, f32[64,8,128,128]{3,2,1,0:T(8,128)}, s32[]{:T(128)}, /*index=5*/s32[]{:T(128)}, s32[]{:T(128)}, s32[]{:T(128)}) while((s32[]{:T(128)}, f32[8,128,128]{2,1,0:T(8,128)S(1)}, s32[]{:T(128)}, f32[64,8,128,128]{3,2,1,0:T(8,128)}, s32[]{:T(128)}, ...), condition=%wide.region_3.4_spmd.clone, body=%wide.region_2.3_spmd.clone.sunk | while | flops 393224 | bytes 1573019 | solution.py:20
  356.6 1.2 add_select_fusion.5
  359.1 1.2 add_select_fusion.5
  360.4 1.2 add_select_fusion.5
  362.9 1.2 add_select_fusion.5
  364.2 1.2 add_select_fusion.5
  365.5 1.2 add_select_fusion.5
  366.7 1.2 add_select_fusion.5
  368.0 1.2 add_select_fusion.5
  370.5 1.2 add_select_fusion.5
  373.0 1.2 add_select_fusion.5
  374.3 1.2 add_select_fusion.5
  375.6 1.2 add_select_fusion.5
  378.1 1.2 add_select_fusion.5
  383.1 1.2 add_select_fusion.5
  386.9 1.2 add_select_fusion.5
  388.2 1.2 add_select_fusion.5
  389.4 1.2 add_select_fusion.5
  390.7 1.2 add_select_fusion.5
  392.0 1.2 add_select_fusion.5
  393.3 1.2 add_select_fusion.5
  397.0 1.2 add_select_fusion.5
  400.8 1.2 add_select_fusion.5
  403.3 1.2 add_select_fusion.5
  415.9 1.6 convolution_bitcast_fusion
  417.5 2.8 fusion.4
  420.2 1.4 copy.82
  422.6 5.9 all-to-all-start.6
  428.5 3.1 fusion.20
  433.5 4.4 all-to-all-done.6
  437.9 4.4 all-to-all-start.5
  442.3 186.0 %all-gather.5.cloned.1.call-done = f32[512,128,128]{2,1,0:T(8,128)} async-done(((f32[8,128,128]{2,1,0:T(8,128)}), f32[512,128,128]{2,1,0:T(8,128)}) %all-gather.5.cloned.1.call-update) | async-done | bytes 33554448 | tf_op jit(solution)/shard_map/all_gather | solution.py:11
  628.3 80.1 %while.30 = (s32[]{:T(128)}, f32[8,128,128]{2,1,0:T(8,128)S(1)}, s32[]{:T(128)}, f32[64,8,128,128]{3,2,1,0:T(8,128)}, s32[]{:T(128)}, /*index=5*/s32[]{:T(128)}) while((s32[]{:T(128)}, f32[8,128,128]{2,1,0:T(8,128)S(1)}, s32[]{:T(128)}, f32[64,8,128,128]{3,2,1,0:T(8,128)}, s32[]{:T(128)}, /*index=5*/s32[]{:T(128)}) %tuple.84), condition=%wide.region_1.2_spmd.clone, body=%wide.region_0.1_spmd.clone.sunk | while | flops 393220 | bytes 1572957 | solution.py:20
  628.3 1.3 add_select_fusion.4
  710.5 5.7 all-to-all-start.3
  716.1 1.9 copy.98
  718.8 6.6 all-to-all-done.3
  (147 shorter events, 141.7 us)
Async XLA Ops:
  7.2 12.2 %copy-start.3 = (bf16[32,8192]{1,0:T(8,128)(2,1)S(1)}, bf16[32,8192]{1,0:T(8,128)(2,1)}, u32[]{:S(2)}) copy-start(bf16[32,8192]{1,0:T(8,128)(2,1)} %param.8) | copy-start | bytes 1572868
  9.1 19.6 %all-to-all-start = ((bf16[32,8,1024]{2,0,1:T(8,128)(2,1)}), bf16[32,8,1024]{2,0,1:T(8,128)(2,1)S(1)}, u32[]{:S(2)}, u32[]{:S(2)}) async-start(bf16[32,8,1024]{2,0,1:T(8,128)(2,1)} %bitcast.100), calls=%async_computation | async-start | bytes 1048576 | tf_op jit(solution)/shard_map/all_to_all | solution.py:38
  28.7 13.7 %all-to-all-start.4 = ((bf16[32,8,1024]{2,0,1:T(8,128)(2,1)}), bf16[32,8,1024]{2,0,1:T(8,128)(2,1)S(1)}, u32[]{:S(2)}, u32[]{:S(2)}) async-start(bf16[32,8,1024]{2,0,1:T(8,128)(2,1)} %bitcast.97), calls=%async_computation.4 | async-start | bytes 1048576 | tf_op jit(solution)/shard_map/all_to_all | solution.py:35
  33.1 302.2 %all-gather.7.cloned.1.call-start = ((), (), s32[]{:S(2)}) async-start(), calls=%async_computation.8 | async-start | bytes 34078720 | tf_op jit(solution)/shard_map/all_gather | solution.py:11
  42.6 1.7 copy-start.4
  43.3 6.2 copy-start.5
  45.1 13.7 %all-to-all-start.2 = ((bf16[32,8,1024]{2,0,1:T(8,128)(2,1)}), bf16[32,8,1024]{2,0,1:T(8,128)(2,1)S(1)}, u32[]{:S(2)}, u32[]{:S(2)}) async-start(bf16[32,8,1024]{2,0,1:T(8,128)(2,1)} %bitcast.98), calls=%async_computation.2 | async-start | bytes 1048576 | tf_op jit(solution)/shard_map/all_to_all | solution.py:36
  58.9 13.7 %all-to-all-start.1 = ((bf16[32,8,1024]{2,0,1:T(8,128)(2,1)}), bf16[32,8,1024]{2,0,1:T(8,128)(2,1)S(1)}, u32[]{:S(2)}, u32[]{:S(2)}) async-start(bf16[32,8,1024]{2,0,1:T(8,128)(2,1)} %bitcast.99), calls=%async_computation.1 | async-start | bytes 1048576 | tf_op jit(solution)/shard_map/all_to_all | solution.py:37
  63.2 565.1 %all-gather.5.cloned.1.call-start = ((), (), s32[]{:S(2)}) async-start(), calls=%async_computation.7 | async-start | bytes 34078720 | tf_op jit(solution)/shard_map/all_gather | solution.py:11
  74.4 1.0 copy-start.1
  422.6 15.3 %all-to-all-start.6 = ((bf16[8,32,1024]{2,1,0:T(8,128)(2,1)}), bf16[8,32,1024]{2,1,0:T(8,128)(2,1)}, u32[]{:S(2)}, u32[]{:S(2)}) async-start(bf16[8,32,1024]{2,1,0:T(8,128)(2,1)} %all_to_all.107), calls=%async_computation.6 | async-start | bytes 1048576 | tf_op jit(solution)/shard_map/all_to_all | solution.py:84
  428.5 3.1 copy-start
  437.9 272.5 %all-to-all-start.5 = ((bf16[8,32,1024]{2,1,0:T(8,128)(2,1)}), bf16[8,32,1024]{2,1,0:T(8,128)(2,1)S(1)}, u32[]{:S(2)}, u32[]{:S(2)}) async-start(bf16[8,32,1024]{2,1,0:T(8,128)(2,1)} %all_to_all.103), calls=%async_computation.5 | async-start | bytes 1048576 | tf_op jit(solution)/shard_map/all_to_all | solution.py:83
  628.3 80.1 %copy-start.2 = (f32[8,256,128]{2,1,0:T(8,128)S(1)}, f32[8,256,128]{2,1,0:T(8,128)}, u32[]{:S(2)}) copy-start(f32[8,256,128]{2,1,0:T(8,128)} %fusion.20) | copy-start | bytes 3145732
  710.5 15.0 %all-to-all-start.3 = ((bf16[8,32,1024]{2,1,0:T(8,128)(2,1)}), bf16[8,32,1024]{2,1,0:T(8,128)(2,1)S(1)}, u32[]{:S(2)}, u32[]{:S(2)}) async-start(bf16[8,32,1024]{2,1,0:T(8,128)(2,1)} %all_to_all.96), calls=%async_computation.3 | async-start | bytes 1048576 | tf_op jit(solution)/shard_map/all_to_all | solution.py:82
Sparse Core Ops, SparseCore 0:
  44.4 290.7 all-gather.6
  338.8 289.5 all-gather.4
where the time goes:
time: 740 us; the launch traced here: 733 us
  waiting for transfers between devices  491 us (66%)
  other arithmetic  158 us (21%)
  starting transfers between devices  39.2 us (5%)
  local copies, waits for them, and re-layouts  15.6 us (2%)
  between operations  14.2 us (2%)
  matrix products  12 us (2%)
    all_gather x2, waiting for transfers between devices, carried_in(): everything = lax.all_gather(value, axis)  444 us
    select_n x128, other arithmetic, turn(): return jnp.where(reached, new, before)  157 us
  transfers between devices with their start and end apart: 9, of which 8 were waited for; matrix products, arithmetic and copies ran while one was open for 24% of the time, Pallas kernels for 0%

commit v1 on v0

--- a/solution.py
+++ b/solution.py
@@ -35,7 +35,12 @@
         lax.all_to_all(queries, "head", split_axis=1, concat_axis=0, tiled=True),
         lax.all_to_all(key_vectors, "head", split_axis=1, concat_axis=0, tiled=True),
         lax.all_to_all(value_vectors, "head", split_axis=1, concat_axis=0, tiled=True),
-        lax.all_to_all(out_grad, "head", split_axis=1, concat_axis=0, tiled=True),
+        jnp.concatenate(
+            lax.all_to_all(
+                jnp.stack(jnp.split(out_grad, lax.axis_size("head"), axis=1)), "head", 0, 0
+            ),
+            axis=0,
+        ),
     )
     start = (lax.axis_index("seq") * rows).astype(f32)
     position = jnp.arange(rows, dtype=f32) + start

time: 740 us -> 750 us (1.014)
  local copies, waits for them, and re-layouts: 15.6 us -> 24.4 us
    unnamed x16 -> x23, local copies, waits for them, and re-layouts: 1.5 us -> 11.8 us
where the time goes in v1:
time: 750 us; the launch traced here: 743 us
  waiting for transfers between devices  492 us (66%)
  other arithmetic  158 us (21%)
  starting transfers between devices  39.2 us (5%)
  local copies, waits for them, and re-layouts  24.4 us (3%)
  between operations  14.2 us (2%)
  matrix products  12 us (2%)
    all_gather x2, waiting for transfers between devices, carried_in(): everything = lax.all_gather(value, axis)  444 us
    select_n x128, other arithmetic, turn(): return jnp.where(reached, new, before)  157 us
  transfers between devices with their start and end apart: 9, of which 8 were waited for; matrix products, arithmetic and copies ran while one was open for 24% of the time, Pallas kernels for 0%

profile of v1, /device:TPU:1, one launch (start us, length us, event | category | flops | bytes accessed | tf_op | source)
XLA Modules:
  0.0 743.0 jit_solution(14074551777151623834)
XLA Ops:
  7.2 1.5 bitcast_dynamic-update-slice_fusion.7
  8.7 1.5 bitcast_dynamic-update-slice_fusion.6
  10.2 1.5 bitcast_dynamic-update-slice_fusion.5
  11.7 1.5 bitcast_dynamic-update-slice_fusion.4
  13.1 1.5 bitcast_dynamic-update-slice_fusion.3
  14.6 1.5 bitcast_dynamic-update-slice_fusion.2
  16.1 1.5 bitcast_dynamic-update-slice_fusion.1
  17.5 1.5 bitcast_dynamic-update-slice_fusion
  19.0 10.2 %all-to-all-start = ((bf16[8,32,1024]{2,1,0:T(8,128)(2,1)}), bf16[8,32,1024]{2,1,0:T(8,128)(2,1)S(1)}, u32[]{:S(2)}, u32[]{:S(2)}) async-start(bf16[8,32,1024]{2,1,0:T(8,128)(2,1)} %bitcast_dynamic-update-slice_fusion), calls=%async_computation | async-start | bytes 1048576 | tf_op jit(solution)/shard_map/all_to_all | solution.py:39
  30.1 8.5 %all-to-all-done = bf16[8,32,1024]{2,1,0:T(8,128)(2,1)S(1)} async-done(((bf16[8,32,1024]{2,1,0:T(8,128)(2,1)}), bf16[8,32,1024]{2,1,0:T(8,128)(2,1)S(1)}, u32[]{:S(2)}, u32[]{:S(2)}) %all-to-all-start) | async-done | bytes 524320 | tf_op jit(solution)/shard_map/all_to_all | solution.py:39
  38.6 4.4 all-to-all-start.4
  43.1 9.2 %all-to-all-done.4 = bf16[32,8,1024]{2,0,1:T(8,128)(2,1)S(1)} async-done(((bf16[32,8,1024]{2,0,1:T(8,128)(2,1)}), bf16[32,8,1024]{2,0,1:T(8,128)(2,1)S(1)}, u32[]{:S(2)}, u32[]{:S(2)}) %all-to-all-start.4) | async-done | bytes 524320 | tf_op jit(solution)/shard_map/all_to_all | solution.py:35
  55.0 4.4 all-to-all-start.2
  60.2 8.5 %all-to-all-done.2 = bf16[32,8,1024]{2,0,1:T(8,128)(2,1)S(1)} async-done(((bf16[32,8,1024]{2,0,1:T(8,128)(2,1)}), bf16[32,8,1024]{2,0,1:T(8,128)(2,1)S(1)}, u32[]{:S(2)}, u32[]{:S(2)}) %all-to-all-start.2) | async-done | bytes 524320 | tf_op jit(solution)/shard_map/all_to_all | solution.py:36
  68.7 4.4 all-to-all-start.1
  73.2 9.3 %all-to-all-done.1 = bf16[32,8,1024]{2,0,1:T(8,128)(2,1)S(1)} async-done(((bf16[32,8,1024]{2,0,1:T(8,128)(2,1)}), bf16[32,8,1024]{2,0,1:T(8,128)(2,1)S(1)}, u32[]{:S(2)}, u32[]{:S(2)}) %all-to-all-start.1) | async-done | bytes 524320 | tf_op jit(solution)/shard_map/all_to_all | solution.py:37
  85.3 1.5 convolution_bitcast_fusion.2
  86.7 258.4 %all-gather.7.cloned.1.call-done = f32[512,128,128]{2,1,0:T(8,128)} async-done(((f32[8,128,128]{2,1,0:T(8,128)}), f32[512,128,128]{2,1,0:T(8,128)}) %all-gather.7.cloned.1.call-update) | async-done | bytes 33554448 | tf_op jit(solution)/shard_map/all_gather | solution.py:11
  345.1 80.6 %while.31 = (s32[]{:T(128)}, f32[8,128,128]{2,1,0:T(8,128)S(1)}, s32[]{:T(128)}, f32[64,8,128,128]{3,2,1,0:T(8,128)}, s32[]{:T(128)}, /*index=5*/s32[]{:T(128)}, s32[]{:T(128)}, s32[]{:T(128)}) while((s32[]{:T(128)}, f32[8,128,128]{2,1,0:T(8,128)S(1)}, s32[]{:T(128)}, f32[64,8,128,128]{3,2,1,0:T(8,128)}, s32[]{:T(128)}, ...), condition=%wide.region_3.4_spmd.clone, body=%wide.region_2.3_spmd.clone.sunk | while | flops 393224 | bytes 1573019 | solution.py:20
  366.5 1.2 add_select_fusion.5
  369.0 1.2 add_select_fusion.5
  370.3 1.2 add_select_fusion.5
  372.8 1.2 add_select_fusion.5
  374.1 1.2 add_select_fusion.5
  377.8 1.2 add_select_fusion.5
  384.1 1.2 add_select_fusion.5
  385.4 1.2 add_select_fusion.5
  387.9 1.2 add_select_fusion.5
  393.0 1.2 add_select_fusion.5
  396.8 1.2 add_select_fusion.5
  398.0 1.2 add_select_fusion.5
  399.3 1.2 add_select_fusion.5
  400.6 1.2 add_select_fusion.5
  401.8 1.2 add_select_fusion.5
  403.1 1.2 add_select_fusion.5
  413.2 1.2 add_select_fusion.5
  425.7 1.6 convolution_bitcast_fusion
  427.3 2.7 fusion.4
  430.1 1.4 copy.74
  432.5 5.9 all-to-all-start.6
  438.3 3.0 fusion.21
  443.3 4.3 all-to-all-done.6
  447.7 4.4 all-to-all-start.5
  452.0 186.1 %all-gather.5.cloned.1.call-done = f32[512,128,128]{2,1,0:T(8,128)} async-done(((f32[8,128,128]{2,1,0:T(8,128)}), f32[512,128,128]{2,1,0:T(8,128)}) %all-gather.5.cloned.1.call-update) | async-done | bytes 33554448 | tf_op jit(solution)/shard_map/all_gather | solution.py:11
  638.2 80.1 %while.30 = (s32[]{:T(128)}, f32[8,128,128]{2,1,0:T(8,128)S(1)}, s32[]{:T(128)}, f32[64,8,128,128]{3,2,1,0:T(8,128)}, s32[]{:T(128)}, /*index=5*/s32[]{:T(128)}) while((s32[]{:T(128)}, f32[8,128,128]{2,1,0:T(8,128)S(1)}, s32[]{:T(128)}, f32[64,8,128,128]{3,2,1,0:T(8,128)}, s32[]{:T(128)}, /*index=5*/s32[]{:T(128)}) %tuple.84), condition=%wide.region_1.2_spmd.clone, body=%wide.region_0.1_spmd.clone.sunk | while | flops 393220 | bytes 1572957 | solution.py:20
  638.2 1.3 add_select_fusion.4
  720.3 5.7 all-to-all-start.3
  727.6 7.7 %all-to-all-done.3 = bf16[8,32,1024]{2,1,0:T(8,128)(2,1)S(1)} async-done(((bf16[8,32,1024]{2,1,0:T(8,128)(2,1)}), bf16[8,32,1024]{2,1,0:T(8,128)(2,1)S(1)}, u32[]{:S(2)}, u32[]{:S(2)}) %all-to-all-start.3) | async-done | bytes 524320 | tf_op jit(solution)/shard_map/all_to_all | solution.py:87
  (153 shorter events, 149.6 us)
Async XLA Ops:
  7.2 22.1 %copy-start.3 = (bf16[32,8192]{1,0:T(8,128)(2,1)S(1)}, bf16[32,8192]{1,0:T(8,128)(2,1)}, u32[]{:S(2)}) copy-start(bf16[32,8192]{1,0:T(8,128)(2,1)} %param.8) | copy-start | bytes 1572868
  19.0 19.6 %all-to-all-start = ((bf16[8,32,1024]{2,1,0:T(8,128)(2,1)}), bf16[8,32,1024]{2,1,0:T(8,128)(2,1)S(1)}, u32[]{:S(2)}, u32[]{:S(2)}) async-start(bf16[8,32,1024]{2,1,0:T(8,128)(2,1)} %bitcast_dynamic-update-slice_fusion), calls=%async_computation | async-start | bytes 1048576 | tf_op jit(solution)/shard_map/all_to_all | solution.py:39
  38.6 13.7 %all-to-all-start.4 = ((bf16[32,8,1024]{2,0,1:T(8,128)(2,1)}), bf16[32,8,1024]{2,0,1:T(8,128)(2,1)S(1)}, u32[]{:S(2)}, u32[]{:S(2)}) async-start(bf16[32,8,1024]{2,0,1:T(8,128)(2,1)} %bitcast.112), calls=%async_computation.4 | async-start | bytes 1048576 | tf_op jit(solution)/shard_map/all_to_all | solution.py:35
  43.0 302.1 %all-gather.7.cloned.1.call-start = ((), (), s32[]{:S(2)}) async-start(), calls=%async_computation.8 | async-start | bytes 34078720 | tf_op jit(solution)/shard_map/all_gather | solution.py:11
  52.5 1.7 copy-start.4
  53.1 6.2 copy-start.5
  55.0 13.7 %all-to-all-start.2 = ((bf16[32,8,1024]{2,0,1:T(8,128)(2,1)}), bf16[32,8,1024]{2,0,1:T(8,128)(2,1)S(1)}, u32[]{:S(2)}, u32[]{:S(2)}) async-start(bf16[32,8,1024]{2,0,1:T(8,128)(2,1)} %bitcast.113), calls=%async_computation.2 | async-start | bytes 1048576 | tf_op jit(solution)/shard_map/all_to_all | solution.py:36
  68.7 13.7 %all-to-all-start.1 = ((bf16[32,8,1024]{2,0,1:T(8,128)(2,1)}), bf16[32,8,1024]{2,0,1:T(8,128)(2,1)S(1)}, u32[]{:S(2)}, u32[]{:S(2)}) async-start(bf16[32,8,1024]{2,0,1:T(8,128)(2,1)} %bitcast.114), calls=%async_computation.1 | async-start | bytes 1048576 | tf_op jit(solution)/shard_map/all_to_all | solution.py:37
  73.1 565.1 %all-gather.5.cloned.1.call-start = ((), (), s32[]{:S(2)}) async-start(), calls=%async_computation.7 | async-start | bytes 34078720 | tf_op jit(solution)/shard_map/all_gather | solution.py:11
  84.3 1.0 copy-start.1
  432.5 15.2 %all-to-all-start.6 = ((bf16[8,32,1024]{2,1,0:T(8,128)(2,1)}), bf16[8,32,1024]{2,1,0:T(8,128)(2,1)S(1)}, u32[]{:S(2)}, u32[]{:S(2)}) async-start(bf16[8,32,1024]{2,1,0:T(8,128)(2,1)} %all_to_all.99), calls=%async_computation.6 | async-start | bytes 1048576 | tf_op jit(solution)/shard_map/all_to_all | solution.py:89
  438.3 3.0 copy-start
  447.7 272.6 %all-to-all-start.5 = ((bf16[8,32,1024]{2,1,0:T(8,128)(2,1)}), bf16[8,32,1024]{2,1,0:T(8,128)(2,1)S(1)}, u32[]{:S(2)}, u32[]{:S(2)}) async-start(bf16[8,32,1024]{2,1,0:T(8,128)(2,1)} %all_to_all.95), calls=%async_computation.5 | async-start | bytes 1048576 | tf_op jit(solution)/shard_map/all_to_all | solution.py:88
  638.2 80.1 %copy-start.2 = (f32[8,256,128]{2,1,0:T(8,128)S(1)}, f32[8,256,128]{2,1,0:T(8,128)}, u32[]{:S(2)}) copy-start(f32[8,256,128]{2,1,0:T(8,128)} %fusion.21) | copy-start | bytes 3145732
  720.3 15.0 %all-to-all-start.3 = ((bf16[8,32,1024]{2,1,0:T(8,128)(2,1)}), bf16[8,32,1024]{2,1,0:T(8,128)(2,1)S(1)}, u32[]{:S(2)}, u32[]{:S(2)}) async-start(bf16[8,32,1024]{2,1,0:T(8,128)(2,1)} %all_to_all.88), calls=%async_computation.3 | async-start | bytes 1048576 | tf_op jit(solution)/shard_map/all_to_all | solution.py:87
Sparse Core Ops, SparseCore 0:
  54.3 290.7 all-gather.6
  348.6 289.5 all-gather.4
